TPU v7x, 32 devices: a whole 2x2x4 slice. The times are simulated.
32 devices in a mesh: dp: 8 (over z, x), expert: 4 (over y, core).
Axes of the slice: x: 2, y: 2, z: 4, core: 2. Of those that a mesh axis runs over, the one named last changes fastest.
Arguments:
- x_spans: bfloat16 [8, 8, 4, 16, 1536], P('dp', None, 'expert'), may hold values from -36 to 36
- crops: int32 [8, 4, 128, 1], P('dp', 'expert'), may hold values from 0 to 7; in each aligned block of 128 rows (0 to 127, 128 to 255, ..., all dimensions but the last counted through in order) at most 32 rows name the same one
- decay: float32 [8, 4, 128, 24], P('dp', 'expert'), may hold values from -1 to 0
- attn_gain: bfloat16 [1536], replicated, may hold values from 0.099609375 to 1.8984375
- w_query: bfloat16 [1536, 1536], replicated, may hold values from -0.15625 to 0.15625
- w_key: bfloat16 [1536, 1536], replicated, may hold values from -0.15625 to 0.15625
- w_value: bfloat16 [1536, 1536], replicated, may hold values from -0.15625 to 0.15625
- head_gain: bfloat16 [1536], replicated, may hold values from 0.099609375 to 1.8984375
- w_out: bfloat16 [1536, 1536], replicated, may hold values from -0.15625 to 0.15625
- moe_gain: bfloat16 [1536], replicated, may hold values from 0.099609375 to 1.8984375
- w_gate: bfloat16 [8, 1536, 6144], P('expert', None, 'dp'), may hold values from -0.15625 to 0.15625
- w_up: bfloat16 [8, 1536, 6144], P('expert', None, 'dp'), may hold values from -0.15625 to 0.15625
- w_down: bfloat16 [8, 6144, 1536], P('expert', 'dp'), may hold values from -0.078125 to 0.078125
Outputs:
- layer_out: bfloat16 [8, 4, 128, 1536], P('dp', 'expert')
Inputs may be any that keep to these rules, and one draw needn't show every extreme that they name: `crops`: within the tokens of one plot no crop is named more than 32 times, and some plot names some crop exactly 32 times.
All inputs are finite; a program needn't handle non-finite values.
Results may differ from a plain program's by a relative error of at most 0.012.
Values may be sent and summed in bfloat16 or wider, within the bound.
A program may use at most 128 MiB of HBM per device.

v0:
```python
import jax
import jax.numpy as jnp
from jax import lax
from jax.sharding import PartitionSpec as P

D = 1536
HEADS = 24
HEAD_DIM = 64
EXPERTS = 8
SPAN = 64


def rms_scale(values, width_eps):
    return lax.rsqrt(jnp.mean(values * values, axis=-1, keepdims=True) + width_eps)


def spread(buffers):
    return lax.all_gather(buffers, "dp", axis=0, tiled=True)


def deliver(buffers):
    return lax.all_to_all(buffers, "expert", split_axis=1, concat_axis=1, tiled=True)


def linear_mixing(query, key_vecs, value_vecs, forget, length):
    blocks = length // SPAN
    query_narrow = query.reshape(blocks, SPAN, HEADS, HEAD_DIM)
    key_narrow = key_vecs.reshape(blocks, SPAN, HEADS, HEAD_DIM)
    query_blocks = query_narrow.astype(jnp.float32)
    key_blocks = key_narrow.astype(jnp.float32)
    value_blocks = value_vecs.astype(jnp.float32).reshape(blocks, SPAN, HEADS, HEAD_DIM)
    within = jnp.cumsum(forget.reshape(blocks, SPAN, HEADS), axis=1)
    block_total = within[:, -1, :]
    scores = jnp.einsum(
        "nthd,nshd->nhts", query_narrow, key_narrow, preferred_element_type=jnp.float32
    )
    by_head = jnp.transpose(within, (0, 2, 1))
    spread_vals = by_head[:, :, :, None] - by_head[:, :, None, :]
    causal = jnp.arange(SPAN)[:, None] >= jnp.arange(SPAN)[None, :]
    weights = jnp.exp(jnp.where(causal[None, None], spread_vals, -jnp.inf))
    local_part = jnp.einsum(
        "nhts,nshd->nthd", scores * weights, value_blocks, precision=lax.Precision.HIGHEST
    )
    carried_keys = key_blocks * jnp.exp(block_total[:, None, :] - within)[..., None]
    block_states = jnp.einsum(
        "nshd,nshe->nhde", carried_keys, value_blocks, precision=lax.Precision.HIGHEST
    )

    def advance(carried, element):
        block_state, total_now = element
        return (carried * jnp.exp(total_now)[:, None, None] + block_state, carried)

    _, entering = lax.scan(
        advance, jnp.zeros((HEADS, HEAD_DIM, HEAD_DIM), jnp.float32), (block_states, block_total)
    )
    earlier_part = jnp.einsum(
        "nthd,nhde->nthe",
        query_blocks * jnp.exp(within)[..., None],
        entering,
        precision=lax.Precision.HIGHEST,
    )
    return (local_part + earlier_part).reshape(length, HEADS, HEAD_DIM)


def on_device(
    x_spans,
    crops,
    decay,
    attn_gain,
    w_query,
    w_key,
    w_value,
    head_gain,
    w_out,
    moe_gain,
    w_gate,
    w_up,
    w_down,
):
    arrived = lax.all_to_all(x_spans, "dp", split_axis=1, concat_axis=0, tiled=True)
    length = arrived.shape[0] * arrived.shape[3]
    tokens = arrived.reshape(length, D)
    forget = decay.reshape(length, HEADS)
    widened = tokens.astype(jnp.float32)
    normed = (widened * rms_scale(widened, 1e-05) * attn_gain.astype(jnp.float32)).astype(
        jnp.bfloat16
    )
    query = jnp.dot(normed, w_query, preferred_element_type=jnp.float32).astype(jnp.bfloat16)
    key_vecs = jnp.dot(normed, w_key, preferred_element_type=jnp.float32).astype(jnp.bfloat16)
    value_vecs = jnp.dot(normed, w_value, preferred_element_type=jnp.float32).astype(jnp.bfloat16)
    mixed = linear_mixing(query, key_vecs, value_vecs, forget, length)
    head_scale = head_gain.astype(jnp.float32).reshape(HEADS, HEAD_DIM)
    head_normed = (
        (mixed * rms_scale(mixed, 1e-05) * head_scale).reshape(length, D).astype(jnp.bfloat16)
    )
    resid = (widened + jnp.dot(head_normed, w_out, preferred_element_type=jnp.float32)).astype(
        jnp.bfloat16
    )
    resid_wide = resid.astype(jnp.float32)
    routed = (resid_wide * rms_scale(resid_wide, 1e-05) * moe_gain.astype(jnp.float32)).astype(
        jnp.bfloat16
    )
    crop_ids = crops.reshape(length)
    onehot = (crop_ids[:, None] == jnp.arange(EXPERTS, dtype=jnp.int32)[None, :]).astype(jnp.int32)
    slot_ids = jnp.sum((jnp.cumsum(onehot, axis=0) - onehot) * onehot, axis=1)
    capacity = length // 4
    position = crop_ids * capacity + slot_ids
    select = (jnp.arange(EXPERTS * capacity, dtype=jnp.int32)[:, None] == position[None, :]).astype(
        jnp.bfloat16
    )
    packed = jnp.dot(select, routed, preferred_element_type=jnp.float32).astype(jnp.bfloat16)
    owners = lax.axis_size("expert")
    local_count = w_gate.shape[0]
    outgoing = packed.reshape(1, owners, EXPERTS * capacity // owners, D)
    gathered = spread(deliver(outgoing))
    sources = gathered.shape[0]
    grouped = gathered.reshape(sources, owners, local_count, capacity, D)
    gate_act = jnp.einsum("sojcd,jdf->sojcf", grouped, w_gate, preferred_element_type=jnp.float32)
    up_act = jnp.einsum("sojcd,jdf->sojcf", grouped, w_up, preferred_element_type=jnp.float32)
    hidden = (jax.nn.silu(gate_act) * up_act).astype(jnp.bfloat16)
    term = jnp.einsum("sojcf,jfd->sojcd", hidden, w_down, preferred_element_type=jnp.float32)
    summed = lax.psum_scatter(
        term.reshape(1 * lax.axis_size("dp"), owners, local_count * capacity, D).astype(
            jnp.bfloat16
        ),
        "dp",
        scatter_dimension=0,
        tiled=True,
    )
    own_sums = summed[0]
    returned = lax.all_to_all(own_sums, "expert", split_axis=0, concat_axis=0, tiled=True)
    flat_back = returned.reshape(EXPERTS * capacity, D)
    expert_out = jnp.einsum("pl,pd->ld", select, flat_back, preferred_element_type=jnp.float32)
    layer_sum = (resid_wide + expert_out).astype(jnp.bfloat16)
    return layer_sum.reshape(1, 1, length, D)


def solution(mesh):
    return jax.shard_map(
        on_device,
        mesh=mesh,
        in_specs=(
            P("dp", None, "expert", None, None),
            P("dp", "expert", None, None),
            P("dp", "expert", None, None),
            P(),
            P(),
            P(),
            P(),
            P(),
            P(),
            P(),
            P("expert", None, "dp"),
            P("expert", None, "dp"),
            P("expert", "dp", None),
        ),
        out_specs=P("dp", "expert", None, None),
        check_vma=False,
    )
```

profile of v0, /device:TPU:0, one launch (start us, length us, event | category | flops | bytes accessed | tf_op | source)
XLA Modules:
  0.0 337.4 jit_solution(17913030399810466076)
XLA Ops:
  6.5 7.3 %all-to-all-start = ((bf16[1,8,1,16,1536]{4,3,2,0,1:T(8,128)(2,1)}), bf16[1,8,1,16,1536]{4,3,2,0,1:T(8,128)(2,1)S(1)}, u32[]{:S(2)}, u32[]{:S(2)}) async-start(bf16[1,8,1,16,1536]{4,3,2,0,1:T(8,128)(2,1)} %bitcast.97), calls=%async_computation | async-start | bytes 786432 | tf_op jit(solution)/shard_map/all_to_all | solution.py:80
  13.8 0.7 fusion.52
  14.6 0.7 convert_element_type.77
  15.3 0.7 convert_element_type.84
  16.7 0.8 copy.77
  20.4 0.8 select_reduce_fusion
  21.2 1.2 multiply_add_fusion
  22.5 3.0 all-to-all-done
  25.9 3.1 convolution_convert_fusion.1
  30.0 3.1 convolution_convert_fusion.2
  33.2 3.1 convolution_convert_fusion.3
  36.3 1.3 reshape.128
  38.1 0.9 copy-done
  39.0 1.5 fusion.45
  40.5 2.2 fusion.24
  42.6 3.8 %while.13 = (s32[]{:T(128)}, f32[24,64,64]{2,1,0:T(8,128)S(1)}, f32[2,24,64,64]{3,2,1,0:T(8,128)}, f32[2,24]{1,0:T(2,128)}, f32[2,24,64,64]{3,2,1,0:T(8,128)S(1)}, /*index=5*/s32[]{:T(128)}, s32[]{:T(128)}) while((s32[]{:T(128)}, f32[24,64,64]{2,1,0:T(8,128)S(1)}, f32[2,24,64,64]{3,2,1,0:T(8,128)}, f32[2,24]{1,0:T(2,128)}, ...), condition=%wide.region_3.4_spmd.clone, body=%wide.region_2.3_spmd.clone.sunk | while | flops 393219 | bytes 2359692 | solution.py:53
  42.8 0.7 fusion.67
  43.6 1.0 bitcast_dynamic-update-slice_fusion.2
  45.4 0.9 bitcast_dynamic-update-slice_fusion.2
  46.5 3.6 %fusion.27 = f32[2,24,64,64]{3,2,1,0:T(8,128)S(1)} fusion(f32[2,24,64,64]{3,2,1,0:T(8,128)} %fusion.45, f32[2,24,64]{2,1,0:T(8,128)} %copy.56, pred[64,64]{1,0:T(8,128)(4,1)} %iota_compare_fusion.4, bf16[2,64,24,64]{3,2,1,0:T(8,128)(2,1)} %reshape.128), kind=kOutput, calls=%fused_computation.38 | convolution fusion | flops 151584768 | bytes 1982464 | tf_op jit(solution)/shard_map/nhts,nshd->nthd/dot_general | solution.py:41
  50.1 3.9 %multiply_reduce_fusion = (f32[2,64,24]{1,2,0:T(8,128)S(1)}, f32[2,64,24,64]{1,3,2,0:T(8,128)S(1)}) fusion(f32[2,24,64,64]{3,2,1,0:T(8,128)S(1)} %fusion.27, f32[2,24,64,64]{3,2,1,0:T(8,128)S(1)} %copy-done.2, f32[2,64,24]{1,2,0:T(8,128)} %copy.63, bf16[2,64,24,64]{3,2,1,0:T(8,128)(2,1)S(1)} %copy-done.1), kind=kOutput, calls=%fused_computation.30 | convolution fusion | flops 151974912 | bytes 2777088 | tf_op jit(solution)/shard_map/nthd,nhde->nthe/dot_general | solution.py:56
  54.2 1.1 copy.67
  56.3 3.5 %multiply_reduce_fusion.1 = (f32[128]{0:T(128)S(1)}, f32[128,1536]{1,0:T(8,128)S(1)}) fusion(bf16[1536,1536]{1,0:T(8,128)(2,1)} %param.23, f32[128,1536]{1,0:T(8,128)S(1)} %reshape.131, f32[128,1536]{1,0:T(8,128)} %copy.67, f32[1536]{0:T(1024)S(1)} %convert_element_type.84, bf16[128,1536]{1,0:T(8,128)(2,1)S(1)} %bitcast.90), kind=kOutput, calls=%fused_computation.47 | convolution fusion | flops 605749120 | bytes 7477760 | tf_op jit(solution)/shard_map/dot_general | solution.py:96
  60.2 14.8 %all_to_all.19 = bf16[1,4,64,1536]{3,2,0,1:T(8,128)(2,1)} all-to-all(bf16[1,4,64,1536]{3,2,0,1:T(8,128)(2,1)S(1)} %bitcast.94), channel_id=1, replica_groups=mesh['dp'=8,'expert'=4] {'expert'}, dimensions={1} | all-to-all | bytes 1572864 | tf_op jit(solution)/shard_map/all_to_all | solution.py:22
  75.1 97.2 %all-gather.2.cloned.1.call-done = bf16[8,4,64,1536]{3,2,1,0:T(8,128)(2,1)} async-done(((bf16[1,4,64,1536]{3,2,1,0:T(8,128)(2,1)}), bf16[8,4,64,1536]{3,2,1,0:T(8,128)(2,1)}) %all-gather.2.cloned.1.call-update) | async-done | bytes 6291472 | tf_op jit(solution)/shard_map/all_gather | solution.py:18
  172.3 8.7 %fusion.6 = f32[2,8,4,32,768]{4,3,2,1,0:T(8,128)S(1)} fusion(bf16[8,4,2,32,1536]{4,3,2,1,0:T(8,128)(2,1)} %bitcast.103, bf16[2,1536,768]{2,1,0:T(8,128)(2,1)} %param.26), kind=kOutput, calls=%fused_computation.13 | convolution fusion | flops 4831838208 | bytes 17301504 | tf_op jit(solution)/shard_map/sojcd,jdf->sojcf/dot_general | solution.py:119
  181.0 8.4 %fusion.2 = bf16[8,4,2,32,768]{4,3,1,0,2:T(8,128)(2,1)S(1)} fusion(f32[2,8,4,32,768]{4,3,2,1,0:T(8,128)S(1)} %fusion.6, bf16[2,1536,768]{2,1,0:T(8,128)(2,1)} %param.25, bf16[8,4,2,32,1536]{4,3,2,1,0:T(8,128)(2,1)S(1)} %bitcast.104), kind=kOutput, calls=%fused_computation.6 | convolution fusion | flops 4841275392 | bytes 20447232 | tf_op jit(solution)/shard_map/sojcd,jdf->sojcf/dot_general | solution.py:118
  189.4 5.2 %convert_bitcast_fusion = bf16[8,4,2,32,1536]{4,3,1,0,2:T(8,128)(2,1)S(1)} fusion(bf16[8,4,2,32,768]{4,3,1,0,2:T(8,128)(2,1)S(1)} %fusion.2, bf16[2,768,1536]{2,1,0:T(8,128)(2,1)S(1)} %bitcast.106), kind=kOutput, calls=%fused_computation.12 | convolution fusion | flops 4834983936 | bytes 14155776 | tf_op jit(solution)/shard_map/sojcf,jfd->sojcd/dot_general | solution.py:121
  194.7 3.4 %copy.72 = bf16[8,4,2,32,1536]{4,3,2,1,0:T(8,128)(2,1)} copy(bf16[8,4,2,32,1536]{4,3,1,0,2:T(8,128)(2,1)S(1)} %convert_bitcast_fusion) | data formatting | bytes 12582912 | tf_op jit(solution)/shard_map/convert_element_type | solution.py:123
  198.1 116.3 %reduce-scatter.2.cloned.1.call-done = bf16[1,4,64,1536]{3,2,1,0:T(8,128)(2,1)} async-done(((bf16[8,4,64,1536]{3,2,1,0:T(8,128)(2,1)}), bf16[1,4,64,1536]{3,2,1,0:T(8,128)(2,1)}) %reduce-scatter.2.cloned.1.call-update) | async-done | bytes 786448 | tf_op jit(solution)/shard_map/reduce_scatter | solution.py:122
  314.4 15.1 %all_to_all.20 = bf16[4,64,1536]{2,1,0:T(8,128)(2,1)S(1)} all-to-all(bf16[4,64,1536]{2,1,0:T(8,128)(2,1)} %bitcast.95), channel_id=1, replica_groups=mesh['dp'=8,'expert'=4] {'expert'}, dimensions={0} | all-to-all | bytes 1572864 | tf_op jit(solution)/shard_map/all_to_all | solution.py:131
  329.5 1.1 fusion.20
  (49 shorter events, 8.1 us)
Async XLA Ops:
  6.5 18.9 %all-to-all-start = ((bf16[1,8,1,16,1536]{4,3,2,0,1:T(8,128)(2,1)}), bf16[1,8,1,16,1536]{4,3,2,0,1:T(8,128)(2,1)S(1)}, u32[]{:S(2)}, u32[]{:S(2)}) async-start(bf16[1,8,1,16,1536]{4,3,2,0,1:T(8,128)(2,1)} %bitcast.97), calls=%async_computation | async-start | bytes 786432 | tf_op jit(solution)/shard_map/all_to_all | solution.py:80
  13.8 158.5 %all-gather.2.cloned.1.call-start = ((), (), s32[]{:S(2)}) async-start(), calls=%async_computation.4 | async-start | bytes 7077888 | tf_op jit(solution)/shard_map/all_gather | solution.py:18
  17.6 8.1 %copy-start.3 = (f32[2,1,24]{2,1,0:T(1,128)}, f32[2,1,24]{2,1,0:T(1,128)S(1)}, u32[]{:S(2)}) copy-start(f32[2,1,24]{2,1,0:T(1,128)S(1)} %slice.4) | copy-start | bytes 580
  38.1 0.9 copy-start
  42.6 7.4 %copy-start.1 = (bf16[2,64,24,64]{3,2,1,0:T(8,128)(2,1)S(1)}, bf16[2,64,24,64]{3,2,1,0:T(8,128)(2,1)}, u32[]{:S(2)}) copy-start(bf16[2,64,24,64]{3,2,1,0:T(8,128)(2,1)} %copy-done) | copy-start | bytes 1179652
  46.5 3.6 %copy-start.2 = (f32[2,24,64,64]{3,2,1,0:T(8,128)S(1)}, f32[2,24,64,64]{3,2,1,0:T(8,128)}, u32[]{:S(2)}) copy-start(f32[2,24,64,64]{3,2,1,0:T(8,128)} %get-tuple-element.32) | copy-start | bytes 2359300
  55.9 3.9 %copy-start.4 = (s32[128]{0:T(128)S(1)}, s32[128]{0:T(128)}, u32[]{:S(2)}) copy-start(s32[128]{0:T(128)} %multiply_add_fusion) | copy-start | bytes 1540
  75.0 239.4 %reduce-scatter.2.cloned.1.call-start = ((), (), s32[]{:S(2)}) async-start(), calls=%async_computation.5 | async-start | bytes 7077888 | tf_op jit(solution)/shard_map/reduce_scatter | solution.py:122
  172.3 8.7 %copy-start.5 = (bf16[8,4,64,1536]{3,2,1,0:T(8,128)(2,1)S(1)}, bf16[8,4,64,1536]{3,2,1,0:T(8,128)(2,1)}, u32[]{:S(2)}) copy-start(bf16[8,4,64,1536]{3,2,1,0:T(8,128)(2,1)} %all-gather.2.cloned.1.call-done) | copy-start | bytes 18874372
  172.3 17.1 %slice-start = ((s8[4718592]{0:T(1024)(128)(4,1)}), s8[4194304]{0:T(1024)(128)(4,1)S(1)}, s32[]{:S(2)}) async-start(s8[4718592]{0:T(1024)(128)(4,1)} %bitcast.105), calls=%async_computation.6 | async-start | bytes 8388608
  181.0 8.4 %slice-start.1 = ((s8[4718592]{0:T(1024)(128)(4,1)}), s8[524288]{0:T(1024)(128)(4,1)S(1)}, s32[]{:S(2)}) async-start(s8[4718592]{0:T(1024)(128)(4,1)} %bitcast.105), calls=%async_computation.7 | async-start | bytes 1048576
Sparse Core Ops, SparseCore 0:
  75.2 97.1 all-gather.1
  198.2 116.1 reduce-scatter.1
where the time goes:
time: 338 us; the launch traced here: 337 us
  waiting for transfers between devices  217 us (64%)
  matrix products  47.8 us (14%)
  blocking collectives  29.9 us (9%)
  between operations  13.7 us (4%)
  local copies, waits for them, and re-layouts  13.6 us (4%)
  other arithmetic  8.3 us (2%)
  starting transfers between devices  7.33 us (2%)
    reduce_scatter x1, waiting for transfers between devices, on_device(): lax.psum_scatter(term.reshape(1 * lax.axis_size('dp'), owners, local_coun...  116 us
    all_gather x1, waiting for transfers between devices, spread(): return lax.all_gather(buffers, 'dp', axis=0, tiled=True)  97.2 us
    all_to_all x1, blocking collectives, on_device(): lax.all_to_all(own_sums, 'expert', split_axis=0, concat_axis=0, tiled=True)  15.1 us
    all_to_all x1, blocking collectives, deliver(): lax.all_to_all(buffers, 'expert', split_axis=1, concat_axis=1, tiled=True)  14.8 us
    dot_general x1, matrix products, on_device(): jnp.einsum('sojcd,jdf->sojcf', grouped, w_up, preferred_element_type=jnp....  8.68 us
    dot_general x1, matrix products, on_device(): jnp.einsum('sojcd,jdf->sojcf', grouped, w_gate, preferred_element_type=jn...  8.37 us
    all_to_all x1, starting transfers between devices, on_device(): lax.all_to_all(x_spans, 'dp', split_axis=1, concat_axis=0, tiled=True)  7.25 us
  transfers between devices with their start and end apart: 3, of which 3 were waited for; matrix products, arithmetic and copies ran while one was open for 3% of the time, Pallas kernels for 0%

commit v1 on v0

--- a/solution.py
+++ b/solution.py
@@ -10,12 +10,34 @@
 SPAN = 64
 
 
+def in_order(parts, dim):
+    parts = jnp.moveaxis(parts, 0, dim)
+    shape = parts.shape
+    return parts.reshape(*shape[:dim], shape[dim] * shape[dim + 1], *shape[dim + 2 :])
+
+
+def collect(shard, axis, dim):
+    devices = lax.axis_size(axis)
+    pairs = [(i, (i + 1) % devices) for i in range(devices)]
+    back = [(b, a) for a, b in pairs]
+    lower, upper = ([], [])
+    for step in range(devices - 1):
+        if step % 2 == 0:
+            lower.append(lax.ppermute(lower[-1] if lower else shard, axis, pairs))
+        else:
+            upper.append(lax.ppermute(upper[-1] if upper else shard, axis, back))
+    blocks = jnp.stack([*lower[::-1], shard, *upper])
+    shift = lax.axis_index(axis) - len(lower)
+    blocks = blocks[(jnp.arange(devices) - shift) % devices]
+    return in_order(blocks, dim)
+
+
 def rms_scale(values, width_eps):
     return lax.rsqrt(jnp.mean(values * values, axis=-1, keepdims=True) + width_eps)
 
 
 def spread(buffers):
-    return lax.all_gather(buffers, "dp", axis=0, tiled=True)
+    return collect(buffers, "dp", 0)
 
 
 def deliver(buffers):

time: 338 us -> 380 us (1.12)
  starting transfers between devices: 7.33 us -> 51.2 us
  local copies, waits for them, and re-layouts: 13.6 us -> 30.9 us
  waiting for transfers between devices: 217 us -> 200 us
    all_gather x1 -> x0, waiting for transfers between devices: 97.2 us -> none  [spread(): return lax.all_gather(buffers, 'dp', axis=0, tiled=True)]
    ppermute x0 -> x7, waiting for transfers between devices: none -> 80.5 us  [the longest x4 80.5 us: collect(): lower.append(lax.ppermute(lower[-1] if lower else shard, axis, pairs))]
    ppermute x0 -> x7, starting transfers between devices: none -> 43.9 us  [the longest x3 37.4 us: collect(): upper.append(lax.ppermute(upper[-1] if upper else shard, axis, back))]
    unnamed x16 -> x33, local copies, waits for them, and re-layouts: 0.89 us -> 11.7 us
    gather x0 -> x1, local copies, waits for them, and re-layouts: none -> 6.39 us  [collect(): blocks = blocks[(jnp.arange(devices) - shift) % devices]]
  transfers between devices with their start and end apart: 3 -> 9, of which waited for: 3 -> 6; matrix products, arithmetic and copies ran while one was open for 3% -> 5% of each run, Pallas kernels for 0% -> 0%
where the time goes in v1:
time: 380 us; the launch traced here: 379 us
  waiting for transfers between devices  200 us (53%)
  starting transfers between devices  51.2 us (13%)
  matrix products  44.9 us (12%)
  local copies, waits for them, and re-layouts  30.9 us (8%)
  blocking collectives  29.4 us (8%)
  between operations  13.8 us (4%)
  other arithmetic  8.98 us (2%)
    reduce_scatter x1, waiting for transfers between devices, on_device(): lax.psum_scatter(term.reshape(1 * lax.axis_size('dp'), owners, local_coun...  117 us
    ppermute x4, waiting for transfers between devices, collect(): lower.append(lax.ppermute(lower[-1] if lower else shard, axis, pairs))  80.5 us
    ppermute x3, starting transfers between devices, collect(): upper.append(lax.ppermute(upper[-1] if upper else shard, axis, back))  37.4 us
    all_to_all x1, blocking collectives, on_device(): lax.all_to_all(own_sums, 'expert', split_axis=0, concat_axis=0, tiled=True)  15.1 us
    all_to_all x1, blocking collectives, deliver(): lax.all_to_all(buffers, 'expert', split_axis=1, concat_axis=1, tiled=True)  14.2 us
    unnamed x33, local copies, waits for them, and re-layouts  11.7 us
    dot_general x1, matrix products, on_device(): jnp.einsum('sojcd,jdf->sojcf', grouped, w_up, preferred_element_type=jnp....  8.68 us
    dot_general x1, matrix products, on_device(): jnp.einsum('sojcd,jdf->sojcf', grouped, w_gate, preferred_element_type=jn...  8.37 us
  transfers between devices with their start and end apart: 9, of which 6 were waited for; matrix products, arithmetic and copies ran while one was open for 5% of the time, Pallas kernels for 0%

profile of v1, /device:TPU:0, one launch (start us, length us, event | category | flops | bytes accessed | tf_op | source)
XLA Modules:
  0.0 379.5 jit_solution(2762869376424258999)
XLA Ops:
  6.5 7.3 %all-to-all-start = ((bf16[1,8,1,16,1536]{4,3,2,0,1:T(8,128)(2,1)}), bf16[1,8,1,16,1536]{4,3,2,0,1:T(8,128)(2,1)S(1)}, u32[]{:S(2)}, u32[]{:S(2)}) async-start(bf16[1,8,1,16,1536]{4,3,2,0,1:T(8,128)(2,1)} %bitcast.118), calls=%async_computation | async-start | bytes 786432 | tf_op jit(solution)/shard_map/all_to_all | solution.py:102
  22.9 2.6 all-to-all-done
  25.9 3.3 convolution_convert_fusion.1
  30.2 3.1 convolution_convert_fusion.3
  34.7 2.2 fusion.24
  36.8 3.8 %while.13 = (s32[]{:T(128)}, f32[24,64,64]{2,1,0:T(8,128)S(1)}, f32[2,24,64,64]{3,2,1,0:T(8,128)}, f32[2,24]{1,0:T(2,128)}, f32[2,24,64,64]{3,2,1,0:T(8,128)S(1)}, /*index=5*/s32[]{:T(128)}, s32[]{:T(128)}) while((s32[]{:T(128)}, f32[24,64,64]{2,1,0:T(8,128)S(1)}, f32[2,24,64,64]{3,2,1,0:T(8,128)}, f32[2,24]{1,0:T(2,128)}, ...), condition=%wide.region_3.4_spmd.clone, body=%wide.region_2.3_spmd.clone.sunk | while | flops 393219 | bytes 2360192 | solution.py:75
  40.7 3.3 convolution_convert_fusion.2
  44.8 1.9 fusion.27
  46.7 3.8 multiply_reduce_fusion
  52.6 3.2 multiply_reduce_fusion.1
  56.3 14.2 %all_to_all.19 = bf16[1,4,64,1536]{3,2,0,1:T(8,128)(2,1)S(1)} all-to-all(bf16[1,4,64,1536]{3,2,0,1:T(8,128)(2,1)S(1)} %bitcast.115), channel_id=1, replica_groups=mesh['dp'=8,'expert'=4] {'expert'}, dimensions={1} | all-to-all | bytes 1572864 | tf_op jit(solution)/shard_map/all_to_all | solution.py:44
  70.6 1.5 collective-permute-start
  72.1 20.1 %collective-permute-done = bf16[1,4,64,1536]{3,2,1,0:T(8,128)(2,1)S(1)} collective-permute-done((bf16[1,4,64,1536]{3,2,1,0:T(8,128)(2,1)S(1)}, bf16[1,4,64,1536]{3,2,1,0:T(8,128)(2,1)S(1)}, u32[]{:S(2)}, u32[]{:S(2)}) %collective-permute-start) | collective-permute-done | bytes 786464 | tf_op jit(solution)/shard_map/ppermute | solution.py:26
  92.2 4.7 %collective-permute-start.4 = (bf16[1,4,64,1536]{3,2,0,1:T(8,128)(2,1)S(1)}, bf16[1,4,64,1536]{3,2,0,1:T(8,128)(2,1)S(1)}, u32[]{:S(2)}, u32[]{:S(2)}) collective-permute-start(bf16[1,4,64,1536]{3,2,0,1:T(8,128)(2,1)S(1)} %all_to_all.19), channel_id=1, source_target_pairs={{4,0},{8,4},{12,8},{16,12},{20,16},{24,20},{28,24},{0,28},{5,1},{9... | collective-permute-start | bytes 2359304 | tf_op jit(solution)/shard_map/ppermute | solution.py:28
  96.9 27.9 %collective-permute-done.1 = bf16[1,4,64,1536]{3,2,1,0:T(8,128)(2,1)S(1)} collective-permute-done((bf16[1,4,64,1536]{3,2,1,0:T(8,128)(2,1)S(1)}, bf16[1,4,64,1536]{3,2,1,0:T(8,128)(2,1)S(1)}, u32[]{:S(2)}, u32[]{:S(2)}) %collective-permute-start.1) | collective-permute-done | bytes 786464 | tf_op jit(solution)/shard_map/ppermute | solution.py:26
  124.8 2.5 collective-permute-start.2
  127.3 15.9 %collective-permute-start.5 = (bf16[1,4,64,1536]{3,2,0,1:T(8,128)(2,1)S(1)}, bf16[1,4,64,1536]{3,2,0,1:T(8,128)(2,1)}, u32[]{:S(2)}, u32[]{:S(2)}) collective-permute-start(bf16[1,4,64,1536]{3,2,0,1:T(8,128)(2,1)S(1)} %collective-permute-done.4), channel_id=1, source_target_pairs={{4,0},{8,4},{12,8},{16,12},{20,16},{24,20},{28,24},{0,28},{5,1},{9... | collective-permute-start | bytes 2359304 | tf_op jit(solution)/shard_map/ppermute | solution.py:28
  143.2 16.9 %collective-permute-done.2 = bf16[1,4,64,1536]{3,2,1,0:T(8,128)(2,1)} collective-permute-done((bf16[1,4,64,1536]{3,2,1,0:T(8,128)(2,1)S(1)}, bf16[1,4,64,1536]{3,2,1,0:T(8,128)(2,1)}, u32[]{:S(2)}, u32[]{:S(2)}) %collective-permute-start.2) | collective-permute-done | bytes 786464 | tf_op jit(solution)/shard_map/ppermute | solution.py:26
  160.2 2.6 collective-permute-start.3
  162.8 16.8 %collective-permute-start.6 = (bf16[1,4,64,1536]{3,2,0,1:T(8,128)(2,1)}, bf16[1,4,64,1536]{3,2,0,1:T(8,128)(2,1)S(1)}, u32[]{:S(2)}, u32[]{:S(2)}) collective-permute-start(bf16[1,4,64,1536]{3,2,0,1:T(8,128)(2,1)} %collective-permute-done.5), channel_id=1, source_target_pairs={{4,0},{8,4},{12,8},{16,12},{20,16},{24,20},{28,24},{0,28},{5,1},{9... | collective-permute-start | bytes 2359304 | tf_op jit(solution)/shard_map/ppermute | solution.py:28
  179.5 15.5 %collective-permute-done.3 = bf16[1,4,64,1536]{3,2,1,0:T(8,128)(2,1)} collective-permute-done((bf16[1,4,64,1536]{3,2,1,0:T(8,128)(2,1)}, bf16[1,4,64,1536]{3,2,1,0:T(8,128)(2,1)}, u32[]{:S(2)}, u32[]{:S(2)}) %collective-permute-start.3) | collective-permute-done | bytes 786464 | tf_op jit(solution)/shard_map/ppermute | solution.py:26
  195.0 2.1 bitcast_dynamic-update-slice_fusion.8
  197.1 2.1 bitcast_dynamic-update-slice_fusion.7
  199.2 2.1 bitcast_dynamic-update-slice_fusion.6
  204.1 2.1 bitcast_dynamic-update-slice_fusion.2
  207.1 6.4 %gather_fusion = bf16[8,4,64,1536]{3,2,1,0:T(8,128)(2,1)} fusion(bf16[8,4,64,1536]{3,2,1,0:T(8,128)(2,1)} %bitcast.19, s32[1024]{0:T(1024)S(1)} %pad_clamp_fusion), kind=kCustom, calls=%fused_computation | custom fusion | bytes 12582944 | tf_op jit(solution)/shard_map/gather | solution.py:31
  213.5 8.7 %fusion.6 = f32[2,8,4,32,768]{4,3,2,1,0:T(8,128)S(1)} fusion(bf16[8,4,2,32,1536]{4,3,2,1,0:T(8,128)(2,1)} %bitcast.110, bf16[2,1536,768]{2,1,0:T(8,128)(2,1)} %param.26), kind=kOutput, calls=%fused_computation.14 | convolution fusion | flops 4831838208 | bytes 17301504 | tf_op jit(solution)/shard_map/sojcd,jdf->sojcf/dot_general | solution.py:141
  222.2 8.4 %fusion.2 = bf16[8,4,2,32,768]{4,3,1,0,2:T(8,128)(2,1)S(1)} fusion(f32[2,8,4,32,768]{4,3,2,1,0:T(8,128)S(1)} %fusion.6, bf16[2,1536,768]{2,1,0:T(8,128)(2,1)} %param.25, bf16[8,4,2,32,1536]{4,3,2,1,0:T(8,128)(2,1)S(1)} %bitcast.111), kind=kOutput, calls=%fused_computation.7 | convolution fusion | flops 4841275392 | bytes 20447232 | tf_op jit(solution)/shard_map/sojcd,jdf->sojcf/dot_general | solution.py:140
  230.6 5.2 %convert_bitcast_fusion = bf16[8,4,2,32,1536]{4,3,1,0,2:T(8,128)(2,1)S(1)} fusion(bf16[8,4,2,32,768]{4,3,1,0,2:T(8,128)(2,1)S(1)} %fusion.2, bf16[2,768,1536]{2,1,0:T(8,128)(2,1)S(1)} %bitcast.125), kind=kOutput, calls=%fused_computation.13 | convolution fusion | flops 4834983936 | bytes 14155776 | tf_op jit(solution)/shard_map/sojcf,jfd->sojcd/dot_general | solution.py:143
  235.9 3.4 copy.72
  239.3 117.1 %reduce-scatter.2.cloned.1.call-done = bf16[1,4,64,1536]{3,2,1,0:T(8,128)(2,1)} async-done(((bf16[8,4,64,1536]{3,2,1,0:T(8,128)(2,1)}), bf16[1,4,64,1536]{3,2,1,0:T(8,128)(2,1)}) %reduce-scatter.2.cloned.1.call-update) | async-done | bytes 786448 | tf_op jit(solution)/shard_map/reduce_scatter | solution.py:144
  356.5 15.1 %all_to_all.20 = bf16[4,64,1536]{2,1,0:T(8,128)(2,1)S(1)} all-to-all(bf16[4,64,1536]{2,1,0:T(8,128)(2,1)} %bitcast.116), channel_id=1, replica_groups=mesh['dp'=8,'expert'=4] {'expert'}, dimensions={0} | all-to-all | bytes 1572864 | tf_op jit(solution)/shard_map/all_to_all | solution.py:153
  (81 shorter events, 23.7 us)
Async XLA Ops:
  6.5 18.9 %all-to-all-start = ((bf16[1,8,1,16,1536]{4,3,2,0,1:T(8,128)(2,1)}), bf16[1,8,1,16,1536]{4,3,2,0,1:T(8,128)(2,1)S(1)}, u32[]{:S(2)}, u32[]{:S(2)}) async-start(bf16[1,8,1,16,1536]{4,3,2,0,1:T(8,128)(2,1)} %bitcast.118), calls=%async_computation | async-start | bytes 786432 | tf_op jit(solution)/shard_map/all_to_all | solution.py:102
  13.8 342.7 %reduce-scatter.2.cloned.1.call-start = ((), (), s32[]{:S(2)}) async-start(), calls=%async_computation.4 | async-start | bytes 7077888 | tf_op jit(solution)/shard_map/reduce_scatter | solution.py:144
  14.7 0.6 copy-start.8
  25.9 7.4 %copy-start.2 = (bf16[128,1536]{1,0:T(8,128)(2,1)}, bf16[128,1536]{1,0:T(8,128)(2,1)S(1)}, u32[]{:S(2)}) copy-start(bf16[128,1536]{1,0:T(8,128)(2,1)S(1)} %fusion.35) | copy-start | bytes 1179652
  40.6 4.2 %copy-start = (bf16[2,64,24,64]{3,2,1,0:T(8,128)(2,1)S(1)}, bf16[2,64,24,64]{3,2,1,0:T(8,128)(2,1)}, u32[]{:S(2)}) copy-start(bf16[2,64,24,64]{3,2,1,0:T(8,128)(2,1)} %reshape.174) | copy-start | bytes 1179652
  40.6 4.2 %copy-start.5 = (f32[2,24,64]{2,1,0:T(8,128)S(1)}, f32[2,24,64]{2,1,0:T(8,128)}, u32[]{:S(2)}) copy-start(f32[2,24,64]{2,1,0:T(8,128)} %copy.56) | copy-start | bytes 36868
  40.7 4.2 %copy-start.7 = (pred[64,64]{1,0:T(8,128)(4,1)S(1)}, pred[64,64]{1,0:T(8,128)(4,1)}, u32[]{:S(2)}) copy-start(pred[64,64]{1,0:T(8,128)(4,1)} %iota_compare_fusion.4) | copy-start | bytes 12292
  44.4 2.3 copy-start.3
  44.4 2.3 copy-start.6
  52.4 3.5 copy-start.9
  70.6 21.6 %collective-permute-start = (bf16[1,4,64,1536]{3,2,1,0:T(8,128)(2,1)S(1)}, bf16[1,4,64,1536]{3,2,1,0:T(8,128)(2,1)S(1)}, u32[]{:S(2)}, u32[]{:S(2)}) collective-permute-start(bf16[1,4,64,1536]{3,2,1,0:T(8,128)(2,1)S(1)} %bitcast.112), channel_id=1, source_target_pairs={{0,4},{4,8},{8,12},{12,16},{16,20},{20,24},{24,28},{28,0},{1,5},{5... | collective-permute-start | bytes 2359304 | tf_op jit(solution)/shard_map/ppermute | solution.py:26
  92.2 32.6 %collective-permute-start.1 = (bf16[1,4,64,1536]{3,2,1,0:T(8,128)(2,1)S(1)}, bf16[1,4,64,1536]{3,2,1,0:T(8,128)(2,1)S(1)}, u32[]{:S(2)}, u32[]{:S(2)}) collective-permute-start(bf16[1,4,64,1536]{3,2,1,0:T(8,128)(2,1)S(1)} %collective-permute-done), channel_id=1, source_target_pairs={{0,4},{4,8},{8,12},{12,16},{16,20},{20,24},{24,28},{28,0},{1,5},{5... | collective-permute-start | bytes 2359304 | tf_op jit(solution)/shard_map/ppermute | solution.py:26
  92.2 35.1 %collective-permute-start.4 = (bf16[1,4,64,1536]{3,2,0,1:T(8,128)(2,1)S(1)}, bf16[1,4,64,1536]{3,2,0,1:T(8,128)(2,1)S(1)}, u32[]{:S(2)}, u32[]{:S(2)}) collective-permute-start(bf16[1,4,64,1536]{3,2,0,1:T(8,128)(2,1)S(1)} %all_to_all.19), channel_id=1, source_target_pairs={{4,0},{8,4},{12,8},{16,12},{20,16},{24,20},{28,24},{0,28},{5,1},{9... | collective-permute-start | bytes 2359304 | tf_op jit(solution)/shard_map/ppermute | solution.py:28
  124.8 2.5 copy-start.4
  124.8 35.3 %collective-permute-start.2 = (bf16[1,4,64,1536]{3,2,1,0:T(8,128)(2,1)S(1)}, bf16[1,4,64,1536]{3,2,1,0:T(8,128)(2,1)}, u32[]{:S(2)}, u32[]{:S(2)}) collective-permute-start(bf16[1,4,64,1536]{3,2,1,0:T(8,128)(2,1)S(1)} %collective-permute-done.1), channel_id=1, source_target_pairs={{0,4},{4,8},{8,12},{12,16},{16,20},{20,24},{24,28},{28,0},{1,5},{5... | collective-permute-start | bytes 2359304 | tf_op jit(solution)/shard_map/ppermute | solution.py:26
  127.3 35.4 %collective-permute-start.5 = (bf16[1,4,64,1536]{3,2,0,1:T(8,128)(2,1)S(1)}, bf16[1,4,64,1536]{3,2,0,1:T(8,128)(2,1)}, u32[]{:S(2)}, u32[]{:S(2)}) collective-permute-start(bf16[1,4,64,1536]{3,2,0,1:T(8,128)(2,1)S(1)} %collective-permute-done.4), channel_id=1, source_target_pairs={{4,0},{8,4},{12,8},{16,12},{20,16},{24,20},{28,24},{0,28},{5,1},{9... | collective-permute-start | bytes 2359304 | tf_op jit(solution)/shard_map/ppermute | solution.py:28
  160.2 34.9 %collective-permute-start.3 = (bf16[1,4,64,1536]{3,2,1,0:T(8,128)(2,1)}, bf16[1,4,64,1536]{3,2,1,0:T(8,128)(2,1)}, u32[]{:S(2)}, u32[]{:S(2)}) collective-permute-start(bf16[1,4,64,1536]{3,2,1,0:T(8,128)(2,1)} %collective-permute-done.2), channel_id=1, source_target_pairs={{0,4},{4,8},{8,12},{12,16},{16,20},{20,24},{24,28},{28,0},{1,5},{5... | collective-permute-start | bytes 2359304 | tf_op jit(solution)/shard_map/ppermute | solution.py:26
  162.8 43.4 %collective-permute-start.6 = (bf16[1,4,64,1536]{3,2,0,1:T(8,128)(2,1)}, bf16[1,4,64,1536]{3,2,0,1:T(8,128)(2,1)S(1)}, u32[]{:S(2)}, u32[]{:S(2)}) collective-permute-start(bf16[1,4,64,1536]{3,2,0,1:T(8,128)(2,1)} %collective-permute-done.5), channel_id=1, source_target_pairs={{4,0},{8,4},{12,8},{16,12},{20,16},{24,20},{28,24},{0,28},{5,1},{9... | collective-permute-start | bytes 2359304 | tf_op jit(solution)/shard_map/ppermute | solution.py:28
  213.5 8.7 %copy-start.1 = (bf16[8,4,64,1536]{3,2,1,0:T(8,128)(2,1)S(1)}, bf16[8,4,64,1536]{3,2,1,0:T(8,128)(2,1)}, u32[]{:S(2)}) copy-start(bf16[8,4,64,1536]{3,2,1,0:T(8,128)(2,1)} %gather_fusion) | copy-start | bytes 18874372
  213.5 17.1 %slice-start = ((s8[4718592]{0:T(1024)(128)(4,1)}), s8[4194304]{0:T(1024)(128)(4,1)S(1)}, s32[]{:S(2)}) async-start(s8[4718592]{0:T(1024)(128)(4,1)} %bitcast.124), calls=%async_computation.5 | async-start | bytes 8388608
  222.2 8.4 %slice-start.1 = ((s8[4718592]{0:T(1024)(128)(4,1)}), s8[524288]{0:T(1024)(128)(4,1)S(1)}, s32[]{:S(2)}) async-start(s8[4718592]{0:T(1024)(128)(4,1)} %bitcast.124), calls=%async_computation.6 | async-start | bytes 1048576
  239.3 132.3 %copy-start.10 = (s32[128]{0:T(128)S(1)}, s32[128]{0:T(128)}, u32[]{:S(2)}) copy-start(s32[128]{0:T(128)} %multiply_add_fusion) | copy-start | bytes 1540
Sparse Core Ops, SparseCore 0:
  239.4 116.9 reduce-scatter.1
